TPU v7x, 32 devices: a whole 2x2x4 slice. The times are simulated.
32 devices in a mesh: gx: 8 (over z, core), gy: 4 (over y, x).
Axes of the slice: x: 2, y: 2, z: 4, core: 2. Of those that a mesh axis runs over, the one named last changes fastest.
Arguments:
- p_prev: float32 [48, 1024, 512], P(None, 'gx', 'gy'), may hold values from -6 to 6
- p_cur: float32 [48, 1024, 512], P(None, 'gx', 'gy'), may hold values from -6 to 6
- courant: float32 [48, 1024, 512], P(None, 'gx', 'gy'), may hold values from 0.04 to 0.2
- snapshots: bfloat16 [3, 48, 1024, 512], P(None, None, 'gx', 'gy'), may hold values from -6 to 6
- residual: float32 [4, 65536, 128], P(None, ('gx', 'gy')), may hold values from -6 to 6
- rec_owner: int32 [65536, 1], P(('gx', 'gy')), may hold values from 0 to 31; in each aligned block of 2048 rows (0 to 2047, 2048 to 4095, ...) at most 128 rows name the same one
- rec_cell: int32 [65536], P(('gx', 'gy')), may hold values from 0 to 16383
- signs: int32 [4], replicated, may hold values from -1 to 1, as said below
Outputs:
- adjoint_field: float32 [48, 1024, 512], P(None, 'gx', 'gy')
- image: float32 [48, 1024, 512], P(None, 'gx', 'gy')
Inputs may be any that keep to these rules, and one draw needn't show every extreme that they name: `rec_owner`: in the rows of one device no owner is named more than 128 times, a bound that some block reaches. `signs`: each entry is +1 or -1, and both occur.
All inputs are finite; a program needn't handle non-finite values.
Results may differ from a plain program's by a relative error of at most 0.0003.
Values sent between devices are 32-bit elements; how exact they have to be, the bound alone decides.
A program may use at most 128 MiB of HBM per device.

v0:
```python
import math

import jax
import jax.numpy as jnp
from jax import lax
from jax.sharding import PartitionSpec as P

STEPS = 3
NT = 128
RECV_DEPTH = 2


COEFF = (-205.0 / 72.0, 8.0 / 5.0, -1.0 / 5.0, 8.0 / 315.0, -1.0 / 560.0)


def extended(cells, sides, width):
    for axis, dim in sides:
        count = lax.axis_size(axis)
        ends = count - 1
        head = lax.slice_in_dim(cells, 0, width, axis=dim)
        tail = lax.slice_in_dim(cells, cells.shape[dim] - width, cells.shape[dim], axis=dim)
        cells = jnp.concatenate(
            [
                lax.ppermute(tail, axis, [(i, (i + 1) % count) for i in range(ends)]),
                cells,
                lax.ppermute(head, axis, [((i + 1) % count, i) for i in range(ends)]),
            ],
            axis=dim,
        )
    return cells


def laplace(ext):
    depth = ext.shape[0]
    width_a = ext.shape[1] - 8
    width_b = ext.shape[2] - 8
    center = ext[:, 4 : 4 + width_a, 4 : 4 + width_b]
    zpad = jnp.pad(center, ((4, 4), (0, 0), (0, 0)))
    total = 3.0 * COEFF[0] * center
    for i in range(1, 5):
        near = (
            ext[:, 4 + i : 4 + i + width_a, 4 : 4 + width_b]
            + ext[:, 4 - i : 4 - i + width_a, 4 : 4 + width_b]
        )
        near = (
            near
            + ext[:, 4 : 4 + width_a, 4 + i : 4 + i + width_b]
            + ext[:, 4 : 4 + width_a, 4 - i : 4 - i + width_b]
        )
        near = near + zpad[4 + i : 4 + i + depth] + zpad[4 - i : 4 - i + depth]
        total = total + COEFF[i] * near
    return total


def step_table(samples, steps):
    rows = jnp.arange(samples).astype(jnp.float32)[:, None]
    cols = jnp.arange(steps).astype(jnp.float32)[None, :]
    return jnp.cos(math.pi * (cols + 0.5) * (rows + 0.5) / samples) * math.sqrt(2.0 / samples)


def shards(p_prev, p_cur, courant, snapshots, residual, rec_owner, rec_cell, signs):
    depth, tile_x, tile_y = p_cur.shape
    devices = lax.axis_size("gx") * lax.axis_size("gy")
    recv_dev = rec_cell.shape[0]
    slots = 2 * recv_dev // devices
    table = step_table(NT, STEPS)
    encoded = jnp.sum(signs.astype(jnp.float32)[:, None, None] * residual, axis=0)
    owner = rec_owner[:, 0]
    onehot = (owner[:, None] == jnp.arange(devices, dtype=jnp.int32)[None, :]).astype(jnp.bfloat16)
    positions = jnp.arange(recv_dev, dtype=jnp.int32)
    lower = (positions[:, None] > positions[None, :]).astype(jnp.bfloat16)
    before = jnp.dot(lower, onehot, preferred_element_type=jnp.float32)
    ranking = jnp.sum(before * onehot.astype(jnp.float32), axis=1).astype(jnp.int32)
    target = owner * slots + ranking
    cell_buffer = (
        jnp.zeros((devices * slots,), jnp.int32).at[target].set(rec_cell).reshape(devices, slots)
    )
    send_buffer = (
        jnp.zeros((devices * slots, NT), jnp.float32)
        .at[target]
        .set(encoded)
        .reshape(devices, slots, NT)
    )
    got_traces, got_cells = (
        lax.all_to_all(send_buffer, ("gx", "gy"), split_axis=0, concat_axis=0, tiled=True),
        lax.all_to_all(cell_buffer, ("gx", "gy"), split_axis=0, concat_axis=0, tiled=True),
    )
    amps = jnp.dot(got_traces.reshape(devices * slots, NT), table, precision=lax.Precision.HIGHEST)
    cells = got_cells.reshape(devices * slots)
    planes = (
        jnp.zeros((STEPS, tile_x * tile_y), jnp.float32)
        .at[:, cells]
        .add(amps.T)
        .reshape(STEPS, tile_x, tile_y)
    )
    image = jnp.zeros(p_cur.shape, jnp.float32)
    prev, cur = (p_prev, p_cur)
    for k in range(STEPS):
        ext = extended(cur, (("gx", 1), ("gy", 2)), 4)
        nxt = 2.0 * cur - prev + courant * laplace(ext)
        nxt = nxt.at[RECV_DEPTH].add(courant[RECV_DEPTH] * planes[k])
        image = image + snapshots[k].astype(jnp.float32) * nxt
        prev, cur = (cur, nxt)
    return (cur, image)


def solution(mesh):
    placed = (
        P(None, "gx", "gy"),
        P(None, "gx", "gy"),
        P(None, "gx", "gy"),
        P(None, None, "gx", "gy"),
        P(None, ("gx", "gy"), None),
        P(("gx", "gy"), None),
        P(("gx", "gy")),
        P(),
    )
    return jax.shard_map(
        shards,
        mesh=mesh,
        in_specs=placed,
        out_specs=(P(None, "gx", "gy"), P(None, "gx", "gy")),
        check_vma=False,
    )
```

profile of v0, /device:TPU:12, one launch (start us, length us, event | category | flops | bytes accessed | tf_op | source)
XLA Modules:
  0.0 370.9 jit_solution(15697514008937132987)
XLA Ops:
  0.6 0.0 copy-start
  0.7 2.4 fusion.105
  3.1 8.8 %scatter_custom_fusion = s32[4096]{0:T(1024)} fusion(s32[2048]{0:T(1024)S(1)} %bitcast.37, s32[2048]{0:T(1024)} %param.20, s32[]{:T(128)} %constant.96.clone.1), kind=kCustom, calls=%fused_computation.197 | custom fusion | bytes 16896 | tf_op jit(solution)/shard_map/scatter | solution.py:76
  11.8 6.0 %all-to-all-start = ((s32[32,1,128]{2,1,0:T(1,128)}), s32[32,1,128]{2,1,0:T(1,128)S(1)}, u32[]{:S(2)}, u32[]{:S(2)}) async-start(s32[32,1,128]{2,1,0:T(1,128)} %bitcast.3), calls=%async_computation | async-start | bytes 32768 | tf_op jit(solution)/shard_map/all_to_all | solution.py:86
  17.9 2.2 collective-permute-start
  20.1 2.1 collective-permute-start.1
  22.3 0.5 add_multiply_fusion
  22.8 1.9 constant_dynamic-update-slice_fusion.1
  24.7 1.5 copy-done.1
  26.1 1.3 multiply_reduce_fusion
  27.5 0.5 convert_add_fusion
  27.9 7.4 %scatter_custom_fusion.1 = f32[4096,128]{1,0:T(8,128)} fusion(s32[2048]{0:T(1024)} %bitcast.38, f32[2048,128]{1,0:T(8,128)} %multiply_reduce_fusion, f32[]{:T(128)} %constant.91.clone.1), kind=kCustom, calls=%fused_computation.181 | custom fusion | bytes 2097664 | tf_op jit(solution)/shard_map/scatter | solution.py:81
  35.3 5.9 %all-to-all-start.1 = ((f32[32,128,128]{2,1,0:T(8,128)}), f32[32,128,128]{2,1,0:T(8,128)}, u32[]{:S(2)}, u32[]{:S(2)}) async-start(f32[32,128,128]{2,1,0:T(8,128)} %bitcast.33), calls=%async_computation.1 | async-start | bytes 4194304 | tf_op jit(solution)/shard_map/all_to_all | solution.py:85
  41.2 0.6 compare_select_fusion
  41.8 0.0 collective-permute-done
  41.8 0.0 collective-permute-done.1
  41.8 0.4 pad_maximum_fusion.3
  42.2 3.7 %fusion.128 = (f32[48,136,4]{2,1,0:T(8,128)}, f32[48,136,4]{2,1,0:T(8,128)}) fusion(f32[48,136,128]{2,1,0:T(8,128)S(1)} %pad_maximum_fusion.3), kind=kLoop, calls=%fused_computation.216 | loop fusion | bytes 417792 | tf_op jit(solution)/shard_map/slice | solution.py:20
  46.0 3.9 %copy.25 = f32[48,136,4]{1,0,2:T(8,128)} copy(f32[48,136,4]{2,1,0:T(8,128)} %get-tuple-element.51) | data formatting | bytes 208896 | tf_op jit(solution)/shard_map/slice | solution.py:20
  49.9 3.3 copy.27
  53.1 3.4 collective-permute-start.3
  56.5 3.9 %collective-permute-start.2 = (f32[48,136,4]{1,0,2:T(8,128)}, f32[48,136,4]{1,0,2:T(8,128)}, u32[]{:S(2)}, u32[]{:S(2)}) collective-permute-start(f32[48,136,4]{1,0,2:T(8,128)} %copy.25), channel_id=1, source_target_pairs={{1,0},{2,1},{3,2},{5,4},{6,5},{7,6},{9,8},{10,9},{11,10},{13,12},{... | collective-permute-start | bytes 313352 | tf_op jit(solution)/shard_map/ppermute | solution.py:26
  60.4 0.7 constant_dynamic-update-slice_fusion
  61.1 13.2 %collective-permute-done.2 = f32[48,136,4]{1,0,2:T(8,128)} collective-permute-done((f32[48,136,4]{1,0,2:T(8,128)}, f32[48,136,4]{1,0,2:T(8,128)}, u32[]{:S(2)}, u32[]{:S(2)}) %collective-permute-start.2) | collective-permute-done | bytes 104480 | tf_op jit(solution)/shard_map/ppermute | solution.py:26
  74.3 3.3 copy.26
  77.6 3.3 copy.28
  80.9 8.3 %pad_maximum_fusion = (f32[48,136,132]{2,1,0:T(8,128)}, f32[48,136,132]{2,1,0:T(8,128)}) fusion(f32[48,136,4]{2,1,0:T(8,128)} %copy.26, f32[48,4,128]{2,1,0:T(4,128)S(1)} %collective-permute-done, f32[48,128,128]{2,1,0:T(8,128)S(1)} %copy-done, f32[48,4,128]{2,1,0:T(4,128)S(1)} %collective-permute-done.1, f32[48,136,4]{2,1,0:T(8,128)} %copy.28), kind=kLoop, calls=%fused_computation.8 | loop fusion | flops 5170176 | bytes 10444800 | tf_op jit(solution)/shard_map/concatenate | solution.py:22
  89.2 46.6 %fusion.11 = f32[48,128,128]{2,1,0:T(8,128)S(1)} fusion(f32[48,128,128]{2,1,0:T(8,128)} %param.16, f32[48,128,128]{2,1,0:T(8,128)} %param.15, f32[48,4,128]{2,1,0:T(4,128)S(1)} %collective-permute-done.1, f32[48,136,132]{2,1,0:T(8,128)} %get-tuple-element.50, f32[48,136,132]{2,1,0:T(8,128)} %get-tuple-element.49, ...), kind=kLoop, calls=%fused_computation.67 | loop fusion | flops 29097984 | bytes 50429952 | tf_op jit(solution)/shard_map/add | solution.py:100
  135.9 4.8 %fusion.115 = f32[4096,3]{1,0:T(8,128)} fusion(f32[4096,128]{1,0:T(8,128)} %bitcast.7, f32[128]{0:T(128)S(1)} %copy-done.5, f32[3]{0:T(128)S(1)} %copy-done.4), kind=kOutput, calls=%fused_computation.201 | convolution fusion | flops 18875520 | bytes 2146828 | tf_op jit(solution)/shard_map/dot_general | solution.py:88
  140.7 29.7 %scatter_custom_fusion.2 = f32[3,16384]{0,1:T(8,128)} fusion(s32[4096]{0:T(1024)} %bitcast.35, f32[4096,3]{1,0:T(8,128)} %fusion.115, f32[]{:T(128)} %constant.91.clone.1), kind=kCustom, calls=%fused_computation.30 | custom fusion | flops 12288 | bytes 197120 | tf_op jit(solution)/shard_map/scatter-add | solution.py:93
  170.4 19.3 %slice_reduce_fusion = (f32[16384]{0:T(1024)S(1)}, f32[16384]{0:T(1024)S(1)}, f32[16384]{0:T(1024)S(1)}) fusion(f32[3,16384]{0,1:T(8,128)} %scatter_custom_fusion.2), kind=kLoop, calls=%fused_computation.5 | loop fusion | bytes 393216 | tf_op jit(solution)/shard_map/slice | solution.py:101
  189.6 0.9 fusion.112
  190.5 1.9 collective-permute-start.4
  192.5 2.4 collective-permute-start.5
  194.9 3.5 collective-permute-done.5
  198.4 0.4 pad_maximum_fusion.4
  198.8 3.8 %fusion.127 = (f32[48,136,4]{2,1,0:T(8,128)}, f32[48,136,4]{2,1,0:T(8,128)}) fusion(f32[48,136,128]{2,1,0:T(8,128)S(1)} %pad_maximum_fusion.4), kind=kLoop, calls=%fused_computation.215 | loop fusion | bytes 417792 | tf_op jit(solution)/shard_map/slice | solution.py:20
  202.6 3.9 %copy.30 = f32[48,136,4]{1,0,2:T(8,128)} copy(f32[48,136,4]{2,1,0:T(8,128)} %get-tuple-element.47) | data formatting | bytes 208896 | tf_op jit(solution)/shard_map/slice | solution.py:20
  206.5 2.2 collective-permute-start.6
  208.8 3.9 %copy.32 = f32[48,136,4]{1,0,2:T(8,128)} copy(f32[48,136,4]{2,1,0:T(8,128)} %get-tuple-element.48) | data formatting | bytes 208896 | tf_op jit(solution)/shard_map/slice | solution.py:21
  212.7 4.4 %collective-permute-start.7 = (f32[48,136,4]{1,0,2:T(8,128)}, f32[48,136,4]{1,0,2:T(8,128)}, u32[]{:S(2)}, u32[]{:S(2)}) collective-permute-start(f32[48,136,4]{1,0,2:T(8,128)} %copy.32), channel_id=1, source_target_pairs={{0,1},{1,2},{2,3},{4,5},{5,6},{6,7},{8,9},{9,10},{10,11},{12,13},{... | collective-permute-start | bytes 313352 | tf_op jit(solution)/shard_map/ppermute | solution.py:24
  217.1 3.3 copy.31
  220.4 2.7 collective-permute-done.7
  223.2 3.3 copy.33
  226.4 8.3 %pad_maximum_fusion.1 = (f32[48,136,132]{2,1,0:T(8,128)}, f32[48,136,132]{2,1,0:T(8,128)}) fusion(f32[48,136,4]{2,1,0:T(8,128)} %copy.31, f32[48,4,128]{2,1,0:T(4,128)S(1)} %collective-permute-done.4, f32[48,128,128]{2,1,0:T(8,128)S(1)} %fusion.112, f32[48,4,128]{2,1,0:T(4,128)S(1)} %collective-permute-done.5, f32[48,136,4]{2,1,0:T(8,128)} %copy.33), kind=kLoop, calls=%fused_computation.10 | loop fusion | flops 5170176 | bytes 10444800 | tf_op jit(solution)/shard_map/concatenate | solution.py:22
  234.7 31.8 %fusion.29 = f32[48,128,128]{2,1,0:T(8,128)} fusion(f32[48,128,128]{2,1,0:T(8,128)} %param.16, f32[48,128,128]{2,1,0:T(8,128)S(1)} %fusion.112, f32[48,4,128]{2,1,0:T(4,128)S(1)} %collective-permute-done.5, f32[48,4,128]{2,1,0:T(4,128)S(1)} %collective-permute-done.4, f32[48,136,132]{2,1,0:T(8,128)} %get-tuple-element.46, ...), kind=kLoop, calls=%fused_computation.85 | loop fusion | flops 32243712 | bytes 37945344 | tf_op jit(solution)/shard_map/add | solution.py:100
  266.5 1.5 fusion.111
  268.0 1.1 fusion.129
  269.1 1.9 collective-permute-start.8
  271.0 2.4 collective-permute-start.9
  273.4 3.5 collective-permute-done.9
  277.0 2.2 pad_maximum_fusion.5
  279.1 3.8 %fusion.126 = (f32[48,136,4]{2,1,0:T(8,128)}, f32[48,136,4]{2,1,0:T(8,128)}) fusion(f32[48,136,128]{2,1,0:T(8,128)S(1)} %pad_maximum_fusion.5), kind=kLoop, calls=%fused_computation.214 | loop fusion | bytes 417792 | tf_op jit(solution)/shard_map/slice | solution.py:20
  282.9 3.9 %copy.34 = f32[48,136,4]{1,0,2:T(8,128)} copy(f32[48,136,4]{2,1,0:T(8,128)} %get-tuple-element.43) | data formatting | bytes 208896 | tf_op jit(solution)/shard_map/slice | solution.py:20
  286.8 2.1 collective-permute-start.10
  288.9 3.9 %copy.36 = f32[48,136,4]{1,0,2:T(8,128)} copy(f32[48,136,4]{2,1,0:T(8,128)} %get-tuple-element.44) | data formatting | bytes 208896 | tf_op jit(solution)/shard_map/slice | solution.py:21
  292.8 4.7 %collective-permute-start.11 = (f32[48,136,4]{1,0,2:T(8,128)}, f32[48,136,4]{1,0,2:T(8,128)}, u32[]{:S(2)}, u32[]{:S(2)}) collective-permute-start(f32[48,136,4]{1,0,2:T(8,128)} %copy.36), channel_id=1, source_target_pairs={{0,1},{1,2},{2,3},{4,5},{5,6},{6,7},{8,9},{9,10},{10,11},{12,13},{... | collective-permute-start | bytes 313352 | tf_op jit(solution)/shard_map/ppermute | solution.py:24
  297.5 3.3 copy.35
  300.7 1.7 collective-permute-done.11
  302.4 3.3 copy.37
  305.7 10.1 %pad_maximum_fusion.2 = (f32[48,136,132]{2,1,0:T(8,128)}, f32[48,136,132]{2,1,0:T(8,128)}) fusion(f32[48,136,4]{2,1,0:T(8,128)} %copy.35, f32[48,4,128]{2,1,0:T(4,128)S(1)} %collective-permute-done.8, f32[48,128,128]{2,1,0:T(8,128)} %fusion.111, f32[48,4,128]{2,1,0:T(4,128)S(1)} %collective-permute-done.9, f32[48,136,4]{2,1,0:T(8,128)} %copy.37), kind=kLoop, calls=%fused_computation.12 | loop fusion | flops 5170176 | bytes 10444800 | tf_op jit(solution)/shard_map/concatenate | solution.py:22
  315.8 46.0 %fusion.47 = f32[48,128,128]{2,1,0:T(8,128)} fusion(f32[48,128,128]{2,1,0:T(8,128)} %param.16, f32[48,128,128]{2,1,0:T(8,128)} %fusion.111, f32[48,4,128]{2,1,0:T(4,128)S(1)} %collective-permute-done.9, f32[48,4,128]{2,1,0:T(4,128)S(1)} %collective-permute-done.8, f32[48,136,132]{2,1,0:T(8,128)} %get-tuple-element.42, ...), kind=kLoop, calls=%fused_computation.103 | loop fusion | flops 32243712 | bytes 37945344 | tf_op jit(solution)/shard_map/add | solution.py:100
  361.8 1.5 fusion.110
  363.3 7.3 %fusion.102 = f32[48,128,128]{2,1,0:T(8,128)} fusion(f32[48,128,128]{2,1,0:T(8,128)} %fusion.110, f32[48,128,128]{2,1,0:T(8,128)} %fusion.111, f32[48,128,128]{2,1,0:T(8,128)S(1)} %fusion.112, bf16[3,48,128,128]{3,2,1,0:T(8,128)(2,1)} %param.17), kind=kLoop, calls=%fused_computation.175 | loop fusion | flops 6291456 | bytes 17301504 | tf_op jit(solution)/shard_map/add | solution.py:102
  (24 shorter events, 0.1 us)
Async XLA Ops:
  0.6 2.4 copy-start.2
  0.6 17.2 %copy-start = (f32[48,128,128]{2,1,0:T(8,128)S(1)}, f32[48,128,128]{2,1,0:T(8,128)}, u32[]{:S(2)}) copy-start(f32[48,128,128]{2,1,0:T(8,128)} %param.15) | copy-start | bytes 9437188
  3.1 14.8 %copy-start.3 = (s32[2048,1]{0,1:T(1,128)}, s32[2048,1]{0,1:T(1,128)S(1)}, u32[]{:S(2)}) copy-start(s32[2048,1]{0,1:T(1,128)S(1)} %compare_select_fusion.1) | copy-start | bytes 24580
  11.8 23.4 %all-to-all-start = ((s32[32,1,128]{2,1,0:T(1,128)}), s32[32,1,128]{2,1,0:T(1,128)S(1)}, u32[]{:S(2)}, u32[]{:S(2)}) async-start(s32[32,1,128]{2,1,0:T(1,128)} %bitcast.3), calls=%async_computation | async-start | bytes 32768 | tf_op jit(solution)/shard_map/all_to_all | solution.py:86
  17.9 23.9 %collective-permute-start = (f32[48,4,128]{2,1,0:T(4,128)S(1)}, f32[48,4,128]{2,1,0:T(4,128)S(1)}, u32[]{:S(2)}, u32[]{:S(2)}) collective-permute-start(f32[48,4,128]{2,1,0:T(4,128)S(1)} %get-tuple-element.57), channel_id=1, source_target_pairs={{4,0},{8,4},{12,8},{16,12},{20,16},{24,20},{28,24},{5,1},{9,5},{13... | collective-permute-start | bytes 294920 | tf_op jit(solution)/shard_map/ppermute | solution.py:26
  20.1 21.7 %collective-permute-start.1 = (f32[48,4,128]{2,1,0:T(4,128)S(1)}, f32[48,4,128]{2,1,0:T(4,128)S(1)}, u32[]{:S(2)}, u32[]{:S(2)}) collective-permute-start(f32[48,4,128]{2,1,0:T(4,128)S(1)} %get-tuple-element.58), channel_id=1, source_target_pairs={{0,4},{4,8},{8,12},{12,16},{16,20},{20,24},{24,28},{1,5},{5,9},{9,... | collective-permute-start | bytes 294920 | tf_op jit(solution)/shard_map/ppermute | solution.py:24
  22.8 1.9 copy-start.6
  22.8 3.3 copy-start.1
  35.3 100.5 %all-to-all-start.1 = ((f32[32,128,128]{2,1,0:T(8,128)}), f32[32,128,128]{2,1,0:T(8,128)}, u32[]{:S(2)}, u32[]{:S(2)}) async-start(f32[32,128,128]{2,1,0:T(8,128)} %bitcast.33), calls=%async_computation.1 | async-start | bytes 4194304 | tf_op jit(solution)/shard_map/all_to_all | solution.py:85
  53.1 24.4 %collective-permute-start.3 = (f32[48,136,4]{1,0,2:T(8,128)S(1)}, f32[48,136,4]{1,0,2:T(8,128)}, u32[]{:S(2)}, u32[]{:S(2)}) collective-permute-start(f32[48,136,4]{1,0,2:T(8,128)S(1)} %copy.27), channel_id=1, source_target_pairs={{0,1},{1,2},{2,3},{4,5},{5,6},{6,7},{8,9},{9,10},{10,11},{12,13},{... | collective-permute-start | bytes 313352 | tf_op jit(solution)/shard_map/ppermute | solution.py:24
  56.5 17.8 %collective-permute-start.2 = (f32[48,136,4]{1,0,2:T(8,128)}, f32[48,136,4]{1,0,2:T(8,128)}, u32[]{:S(2)}, u32[]{:S(2)}) collective-permute-start(f32[48,136,4]{1,0,2:T(8,128)} %copy.25), channel_id=1, source_target_pairs={{1,0},{2,1},{3,2},{5,4},{6,5},{7,6},{9,8},{10,9},{11,10},{13,12},{... | collective-permute-start | bytes 313352 | tf_op jit(solution)/shard_map/ppermute | solution.py:26
  89.2 46.7 %copy-start.4 = (f32[3]{0:T(128)S(1)}, f32[3]{0:T(128)}, u32[]{:S(2)}) copy-start(f32[3]{0:T(128)} %add_multiply_fusion) | copy-start | bytes 40
  89.2 46.7 %copy-start.5 = (f32[128]{0:T(128)S(1)}, f32[128]{0:T(128)}, u32[]{:S(2)}) copy-start(f32[128]{0:T(128)} %convert_add_fusion) | copy-start | bytes 1540
  190.5 4.3 %collective-permute-start.4 = (f32[48,4,128]{2,1,0:T(4,128)S(1)}, f32[48,4,128]{2,1,0:T(4,128)S(1)}, u32[]{:S(2)}, u32[]{:S(2)}) collective-permute-start(f32[48,4,128]{2,1,0:T(4,128)S(1)} %get-tuple-element.55), channel_id=1, source_target_pairs={{4,0},{8,4},{12,8},{16,12},{20,16},{24,20},{28,24},{5,1},{9,5},{13... | collective-permute-start | bytes 294920 | tf_op jit(solution)/shard_map/ppermute | solution.py:26
  192.5 5.9 %collective-permute-start.5 = (f32[48,4,128]{2,1,0:T(4,128)S(1)}, f32[48,4,128]{2,1,0:T(4,128)S(1)}, u32[]{:S(2)}, u32[]{:S(2)}) collective-permute-start(f32[48,4,128]{2,1,0:T(4,128)S(1)} %get-tuple-element.56), channel_id=1, source_target_pairs={{0,4},{4,8},{8,12},{12,16},{16,20},{20,24},{24,28},{1,5},{5,9},{9,... | collective-permute-start | bytes 294920 | tf_op jit(solution)/shard_map/ppermute | solution.py:24
  206.5 10.6 %collective-permute-start.6 = (f32[48,136,4]{1,0,2:T(8,128)}, f32[48,136,4]{1,0,2:T(8,128)}, u32[]{:S(2)}, u32[]{:S(2)}) collective-permute-start(f32[48,136,4]{1,0,2:T(8,128)} %copy.30), channel_id=1, source_target_pairs={{1,0},{2,1},{3,2},{5,4},{6,5},{7,6},{9,8},{10,9},{11,10},{13,12},{... | collective-permute-start | bytes 313352 | tf_op jit(solution)/shard_map/ppermute | solution.py:26
  212.7 10.5 %collective-permute-start.7 = (f32[48,136,4]{1,0,2:T(8,128)}, f32[48,136,4]{1,0,2:T(8,128)}, u32[]{:S(2)}, u32[]{:S(2)}) collective-permute-start(f32[48,136,4]{1,0,2:T(8,128)} %copy.32), channel_id=1, source_target_pairs={{0,1},{1,2},{2,3},{4,5},{5,6},{6,7},{8,9},{9,10},{10,11},{12,13},{... | collective-permute-start | bytes 313352 | tf_op jit(solution)/shard_map/ppermute | solution.py:24
  269.1 4.3 %collective-permute-start.8 = (f32[48,4,128]{2,1,0:T(4,128)S(1)}, f32[48,4,128]{2,1,0:T(4,128)S(1)}, u32[]{:S(2)}, u32[]{:S(2)}) collective-permute-start(f32[48,4,128]{2,1,0:T(4,128)S(1)} %get-tuple-element.53), channel_id=1, source_target_pairs={{4,0},{8,4},{12,8},{16,12},{20,16},{24,20},{28,24},{5,1},{9,5},{13... | collective-permute-start | bytes 294920 | tf_op jit(solution)/shard_map/ppermute | solution.py:26
  271.0 5.9 %collective-permute-start.9 = (f32[48,4,128]{2,1,0:T(4,128)S(1)}, f32[48,4,128]{2,1,0:T(4,128)S(1)}, u32[]{:S(2)}, u32[]{:S(2)}) collective-permute-start(f32[48,4,128]{2,1,0:T(4,128)S(1)} %get-tuple-element.54), channel_id=1, source_target_pairs={{0,4},{4,8},{8,12},{12,16},{16,20},{20,24},{24,28},{1,5},{5,9},{9,... | collective-permute-start | bytes 294920 | tf_op jit(solution)/shard_map/ppermute | solution.py:24
  286.8 10.6 %collective-permute-start.10 = (f32[48,136,4]{1,0,2:T(8,128)}, f32[48,136,4]{1,0,2:T(8,128)}, u32[]{:S(2)}, u32[]{:S(2)}) collective-permute-start(f32[48,136,4]{1,0,2:T(8,128)} %copy.34), channel_id=1, source_target_pairs={{1,0},{2,1},{3,2},{5,4},{6,5},{7,6},{9,8},{10,9},{11,10},{13,12},{... | collective-permute-start | bytes 313352 | tf_op jit(solution)/shard_map/ppermute | solution.py:26
  292.8 9.7 %collective-permute-start.11 = (f32[48,136,4]{1,0,2:T(8,128)}, f32[48,136,4]{1,0,2:T(8,128)}, u32[]{:S(2)}, u32[]{:S(2)}) collective-permute-start(f32[48,136,4]{1,0,2:T(8,128)} %copy.36), channel_id=1, source_target_pairs={{0,1},{1,2},{2,3},{4,5},{5,6},{6,7},{8,9},{9,10},{10,11},{12,13},{... | collective-permute-start | bytes 313352 | tf_op jit(solution)/shard_map/ppermute | solution.py:24
where the time goes:
time: 378 us; the launch traced here: 371 us
  other arithmetic  198 us (52%)
  local copies, waits for them, and re-layouts  94.4 us (25%)
  starting transfers between devices  45.5 us (12%)
  waiting for transfers between devices  24.7 us (7%)
  matrix products  7.14 us (2%)
    add x3, other arithmetic, shards(): nxt = 2.0 * cur - prev + courant * laplace(ext)  124 us
    scatter-add x1, other arithmetic, shards(): planes = jnp.zeros((STEPS, tile_x * tile_y), jnp.float32).at[:, cells].ad...  29.7 us
    concatenate x6, other arithmetic, extended(): jnp.concatenate([lax.ppermute(tail, axis, [(i, (i + 1) % count) for i in...  29.6 us
    slice x9, local copies, waits for them, and re-layouts, extended(): head = lax.slice_in_dim(cells, 0, width, axis=dim)  24.2 us
    ppermute x6, starting transfers between devices, extended(): lax.ppermute(tail, axis, [(i, (i + 1) % count) for i in range(ends)])  19.4 us
    slice x1, local copies, waits for them, and re-layouts, shards(): nxt = nxt.at[RECV_DEPTH].add(courant[RECV_DEPTH] * planes[k])  19.3 us
    ppermute x6, starting transfers between devices, extended(): lax.ppermute(head, axis, [((i + 1) % count, i) for i in range(ends)])  14.2 us
    ppermute x6, waiting for transfers between devices, extended(): lax.ppermute(head, axis, [((i + 1) % count, i) for i in range(ends)])  13.2 us
  transfers between devices with their start and end apart: 14, of which 5 were waited for; matrix products, arithmetic and copies ran while one was open for 27% of the time, Pallas kernels for 0%

commit v1 on v0

v1 whole, which is shorter than its diff:
```python
import functools
import math

import jax
import jax.numpy as jnp
import numpy as np
from jax import lax
from jax.experimental import pallas as pl
from jax.experimental.pallas import tpu as pltpu
from jax.sharding import PartitionSpec as P

STEPS = 3
NT = 128
RECV_DEPTH = 2
HALO = 4
CHUNK = 16
BLOCK = 256

SCALE = 5040.0
CENTER = -205.0 / 72.0 * SCALE
TAPS = (8064.0, -1008.0, 128.0, -9.0)

F32 = jnp.float32
BF16 = jnp.bfloat16
I32 = jnp.int32
MESH = pl.DeviceIdType.MESH


def taps(distance):
    out = jnp.zeros(distance.shape, F32)
    for i, c in enumerate(TAPS):
        out = jnp.where(distance == i + 1, c, out)
    return out


def split(v, axis):
    hi = v.astype(BF16)
    lo = (v - hi.astype(F32)).astype(BF16)
    return jnp.concatenate([hi, lo], axis=axis)


def iota(shape, dim):
    return lax.broadcasted_iota(I32, shape, dim)


def lanes_dot(a, b, **kw):
    return lax.dot_general(a, b, (((1,), (1,)), ((), ())), preferred_element_type=F32, **kw)


def kernel(
    n_gx, n_gy, signs, owner, cell, table, p_prev, p_cur, courant_h, snaps_h, residual_h,
    field_out, image_out,
    buf_a, buf_b, courant, snaps, residual, image, sx, rx, sy, ry, corner, edge, planes,
    snd, got, load_sem, out_sem, sxs, rxs, sys_, rys, snds, gots,
):
    n = n_gx * n_gy
    nz, nx, ny = p_cur.shape
    half, mid = nx // 2, ny // 2
    chunks = nz // CHUNK
    gx, gy = lax.axis_index("gx"), lax.axis_index("gy")
    me = gx * n_gy + gy

    inner = pl.ds(HALO, nz)
    loads = [
        pltpu.make_async_copy(p_cur, buf_a.at[inner], load_sem.at[0]),
        pltpu.make_async_copy(residual_h, residual, load_sem.at[1]),
        pltpu.make_async_copy(p_prev, buf_b.at[inner], load_sem.at[2]),
        pltpu.make_async_copy(courant_h, courant, load_sem.at[3]),
    ] + [pltpu.make_async_copy(snaps_h.at[k], snaps.at[k], load_sem.at[4 + k]) for k in range(STEPS)]
    for load in loads:
        load.start()

    barrier = pltpu.get_barrier_semaphore()

    def greet(o, carry):
        d = lax.rem(me + o, n)
        pl.semaphore_signal(
            barrier, inc=1, device_id=(d // n_gy, lax.rem(d, n_gy)), device_id_type=MESH
        )
        return carry

    lax.fori_loop(1, n, greet, 0)

    band = taps(jnp.abs(iota((nx, nx), 0) - iota((nx, nx), 1))).astype(BF16)
    t_x = jnp.concatenate([band, band], axis=1)
    t_y = jnp.concatenate([band, band], axis=0) if nx == ny else None
    row = iota((16, 16), 0)
    src = iota((16, 16), 1) & 7
    place = jnp.where(src < 4, src - 4, nx + src - 4)
    target = jnp.where(row < 8, row, nx - 16 + row)
    h_x = taps(jnp.abs(place - target)).astype(BF16)
    a, b = iota((ny, ny), 0), iota((ny, ny), 1)
    pos = jnp.where(a < mid, (a & 3) - 4, ny + (a & 3))
    edge_taps = taps(jnp.abs(b - pos))
    group = (a & (mid - 1)) >> 2

    def fill(q, carry):
        c = jnp.where(group == q, edge_taps, 0.0).astype(BF16)
        corner[q, pl.ds(0, ny), :] = c
        corner[q, pl.ds(ny, ny), :] = c
        return carry

    lax.fori_loop(0, CHUNK, fill, 0)
    zero = jnp.zeros((HALO, nx, ny), F32)
    for buf in (buf_a, buf_b):
        buf[pl.ds(0, HALO)] = zero
        buf[pl.ds(HALO + nz, HALO)] = zero

    for side, absent in ((0, gx == 0), (1, gx == n_gx - 1)):

        @pl.when(absent)
        def _(side=side):
            for k in range(STEPS):
                rx[k, side] = jnp.zeros(rx.shape[2:], F32)

    for side, absent in ((0, gy == 0), (1, gy == n_gy - 1)):

        @pl.when(absent)
        def _(side=side):
            for k in range(STEPS):
                ry[k, side] = jnp.zeros(ry.shape[2:], F32)

    lane = iota((half, ny), 1)

    def pack(v, k, g, q):
        z = g * CHUNK + q
        sx[k, 0, z] = v[nx - HALO :]
        sx[k, 1, z] = v[:HALO]
        top, low = v[:half], v[half:]
        first = (lane >> 2) == q
        second = (lane >> 2) == q + mid // 4
        s = 4 * q
        right = sy[k, 0, g]
        right = jnp.where(first, pltpu.roll(top, s + 4, 1), right)
        right = jnp.where(second, pltpu.roll(low, s + mid + 4, 1), right)
        sy[k, 0, g] = right
        left = sy[k, 1, g]
        left = jnp.where(second, pltpu.roll(top, s + mid, 1), left)
        left = jnp.where(first, pltpu.roll(low, s, 1), left)
        sy[k, 1, g] = left

    def halo_copies(k, g):
        zs = pl.ds(g * CHUNK, CHUNK)
        out = []
        for side, step, send_ok, recv_ok in (
            (0, 1, gx < n_gx - 1, gx > 0),
            (1, -1, gx > 0, gx < n_gx - 1),
        ):
            i = (k * chunks + g) * 2 + side
            copy = pltpu.make_async_remote_copy(
                src_ref=sx.at[k, side, zs], dst_ref=rx.at[k, side, zs],
                send_sem=sxs.at[i], recv_sem=rxs.at[i],
                device_id=(lax.rem(gx + step + n_gx, n_gx), gy), device_id_type=MESH,
            )
            out.append((copy, send_ok, recv_ok))
        for side, step, send_ok, recv_ok in (
            (0, 1, gy < n_gy - 1, gy > 0),
            (1, -1, gy > 0, gy < n_gy - 1),
        ):
            i = (k * chunks + g) * 2 + side
            copy = pltpu.make_async_remote_copy(
                src_ref=sy.at[k, side, g], dst_ref=ry.at[k, side, g],
                send_sem=sys_.at[i], recv_sem=rys.at[i],
                device_id=(gx, lax.rem(gy + step + n_gy, n_gy)), device_id_type=MESH,
            )
            out.append((copy, send_ok, recv_ok))
        return out

    def send_halo(k, g):
        for copy, send_ok, _ in halo_copies(k, g):
            pl.when(send_ok)(copy.start)

    def wait_halo(k, g):
        for copy, _, recv_ok in halo_copies(k, g):
            pl.when(recv_ok)(copy.wait_recv)

    order = tuple(range(1, chunks)) + (0,)

    loads[0].wait()
    for g in order:

        def first_pack(q, carry, g=g):
            pack(buf_a[HALO + g * CHUNK + q], 0, g, q)
            return carry

        lax.fori_loop(0, CHUNK, first_pack, 0)
    pl.semaphore_wait(barrier, n - 1)
    for g in order:
        send_halo(0, g)

    loads[1].wait()
    recv_dev = owner.shape[1]
    slots = snd.shape[2]
    upper = (iota((BLOCK, BLOCK), 0) < iota((BLOCK, BLOCK), 1)).astype(F32).astype(BF16)
    count = jnp.zeros((n, 1), F32)
    message = jnp.zeros((n * 8, slots), F32)
    part = iota((8, BLOCK), 0)
    shift = ny.bit_length() - 1
    for blk in range(recv_dev // BLOCK):
        rows = pl.ds(blk * BLOCK, BLOCK)
        enc = signs[0].astype(F32) * residual[0, rows, :]
        for s in range(1, residual.shape[0]):
            enc = enc + signs[s].astype(F32) * residual[s, rows, :]
        amps = lanes_dot(table[...], enc, precision=lax.Precision.HIGHEST)
        hi = amps.astype(BF16).astype(F32)
        c = cell[:, rows]
        at_x = (c >> shift).astype(F32)
        at_y = (c & (ny - 1)).astype(F32)
        payload = jnp.where((part & 1) == 0, hi, amps - hi)
        payload = jnp.where(part == 6, at_x, payload)
        payload = jnp.where(part == 7, at_y, payload)
        onehot = jnp.where(iota((n, BLOCK), 0) == owner[:, rows], 1.0, 0.0)
        before = jnp.dot(onehot.astype(BF16), upper, preferred_element_type=F32) + count
        count = count + jnp.sum(onehot, axis=1, keepdims=True)
        rank = jnp.sum(before * onehot, axis=0, keepdims=True)
        spread = (onehot[:, None, :] * payload[None]).reshape(n * 8, BLOCK).astype(BF16)
        slot = jnp.where(iota((slots, BLOCK), 0).astype(F32) == rank, 1.0, 0.0).astype(BF16)
        message = message + lanes_dot(spread, slot)
    snd[...] = message.reshape(n, 8, slots)
    got[me] = snd[me]

    def message_to(o):
        d = lax.rem(me + o, n)
        return pltpu.make_async_remote_copy(
            src_ref=snd.at[d], dst_ref=got.at[me], send_sem=snds.at[o], recv_sem=gots.at[o],
            device_id=(d // n_gy, lax.rem(d, n_gy)), device_id_type=MESH,
        )

    def post(o, carry):
        message_to(o).start()
        return carry

    lax.fori_loop(1, n, post, 0)

    def step_chunk(k, g, cur, prev):
        wait_halo(k, g)
        left, right = ry[k, 0, g], ry[k, 1, g]
        near = lane < mid
        edges = jnp.concatenate(
            [jnp.where(near, left, right), pltpu.roll(jnp.where(near, right, left), mid, 1)], axis=0
        )
        edge[...] = split(edges, 1)

        def plane(q):
            z = g * CHUNK + q
            v = cur[z + HALO]
            lap = jnp.dot(split(v, 1), t_y, preferred_element_type=F32)
            lap = lap + jnp.dot(edge[...], corner[q], preferred_element_type=F32)
            lap = lap + jnp.dot(t_x, split(v, 0), preferred_element_type=F32)
            over = jnp.concatenate([rx[k, 0, z], rx[k, 1, z]], axis=0)
            over_hi = over.astype(BF16).astype(F32)
            over = jnp.concatenate([over_hi, over - over_hi], axis=0).astype(BF16)
            border = jnp.dot(h_x, over, preferred_element_type=F32)
            depth = (3.0 * CENTER) * v
            for i in range(1, HALO + 1):
                depth = depth + TAPS[i - 1] * (cur[z + HALO + i] + cur[z + HALO - i])
            lap = lap + depth
            lap = jnp.concatenate(
                [lap[:8] + border[:8], lap[8 : nx - 8], lap[nx - 8 :] + border[8:]], axis=0
            )
            nxt = (2.0 * v - prev[z + HALO]) + (courant[z] * (1.0 / SCALE)) * lap
            prev[z + HALO] = nxt
            shot = snaps[k, z].astype(F32) * nxt
            image[z] = shot if k == 0 else image[z] + shot
            if k < STEPS - 1:
                pack(nxt, k + 1, g, q)

        def body(j, carry):
            plane(2 * j)
            plane(2 * j + 1)
            return carry

        lax.fori_loop(0, CHUNK // 2, body, 0)
        if k < STEPS - 1:
            send_halo(k + 1, g)

    def scatter():
        def arrive(o, carry):
            d = lax.rem(me - o + n, n)
            pltpu.make_async_remote_copy(
                src_ref=snd.at[d], dst_ref=got.at[d], send_sem=snds.at[o], recv_sem=gots.at[o],
                device_id=(d // n_gy, lax.rem(d, n_gy)), device_id_type=MESH,
            ).wait_recv()
            return carry

        lax.fori_loop(1, n, arrive, 0)
        planes[...] = jnp.zeros(planes.shape, F32)
        row_x = iota((nx, slots), 0).astype(F32)
        row_y = iota((ny, slots), 0).astype(F32)

        def gather(j, carry):
            lhs = [[] for _ in range(STEPS)]
            rhs = []
            for i in range(4):
                block = got[4 * j + i]
                at_x = row_x == block[6:7]
                at_y = jnp.where(row_y == block[7:8], 1.0, 0.0).astype(BF16)
                for k in range(STEPS):
                    for h in range(2):
                        lhs[k].append(
                            jnp.where(at_x, block[2 * k + h : 2 * k + h + 1], 0.0).astype(BF16)
                        )
                rhs += [at_y, at_y]
            lhs = jnp.concatenate([jnp.concatenate(l, axis=1) for l in lhs], axis=0)
            planes[...] += lanes_dot(lhs, jnp.concatenate(rhs, axis=1))
            return carry

        lax.fori_loop(0, n // 4, gather, 0)

    outs = []
    for load in loads[2:]:
        load.wait()
    for k in range(STEPS):
        cur, prev = (buf_a, buf_b) if k % 2 == 0 else (buf_b, buf_a)
        for g in order:
            if g == RECV_DEPTH // CHUNK:
                if k == 0:
                    scatter()
                at = HALO + RECV_DEPTH
                prev[at] = prev[at] - courant[RECV_DEPTH] * planes[pl.ds(k * nx, nx), :]
            step_chunk(k, g, cur, prev)
            if k == STEPS - 1:
                zs = pl.ds(g * CHUNK, CHUNK)
                outs += [
                    pltpu.make_async_copy(
                        prev.at[pl.ds(HALO + g * CHUNK, CHUNK)], field_out.at[zs], out_sem.at[2 * g]
                    ),
                    pltpu.make_async_copy(image.at[zs], image_out.at[zs], out_sem.at[2 * g + 1]),
                ]
                outs[-2].start()
                outs[-1].start()

    def finish(o, carry):
        message_to(o).wait_send()
        return carry

    lax.fori_loop(1, n, finish, 0)
    for k in range(STEPS):
        for g in order:
            for copy, send_ok, _ in halo_copies(k, g):
                pl.when(send_ok)(copy.wait_send)
    for out in outs:
        out.wait()


def step_table(samples, steps):
    rows = np.arange(samples, dtype=np.float64)[None, :]
    cols = np.repeat(np.arange(steps, dtype=np.float64), 2)[:, None]
    table = np.cos(math.pi * (cols + 0.5) * (rows + 0.5) / samples) * math.sqrt(2.0 / samples)
    return np.concatenate([table, np.zeros((8 - 2 * steps, samples))]).astype(np.float32)


def shards(n_gx, n_gy, p_prev, p_cur, courant, snapshots, residual, rec_owner, rec_cell, signs):
    nz, nx, ny = p_cur.shape
    n = n_gx * n_gy
    recv_dev = rec_cell.shape[0]
    slots = -(-(2 * recv_dev // n) // 128) * 128
    chunks = nz // CHUNK
    anywhere = pl.BlockSpec(memory_space=pl.ANY)
    vmem = pl.BlockSpec(memory_space=pltpu.VMEM)
    dma = pltpu.SemaphoreType.DMA
    whole = jax.ShapeDtypeStruct(p_cur.shape, F32)
    return pl.pallas_call(
        functools.partial(kernel, n_gx, n_gy),
        out_shape=(whole, whole),
        in_specs=[pl.BlockSpec(memory_space=pltpu.SMEM)] + [vmem] * 3 + [anywhere] * 5,
        out_specs=(anywhere, anywhere),
        scratch_shapes=[
            pltpu.VMEM((nz + 2 * HALO, nx, ny), F32),
            pltpu.VMEM((nz + 2 * HALO, nx, ny), F32),
            pltpu.VMEM((nz, nx, ny), F32),
            pltpu.VMEM((STEPS, nz, nx, ny), BF16),
            pltpu.VMEM(residual.shape, F32),
            pltpu.VMEM((nz, nx, ny), F32),
            pltpu.VMEM((STEPS, 2, nz, HALO, ny), F32),
            pltpu.VMEM((STEPS, 2, nz, HALO, ny), F32),
            pltpu.VMEM((STEPS, 2, chunks, nx // 2, ny), F32),
            pltpu.VMEM((STEPS, 2, chunks, nx // 2, ny), F32),
            pltpu.VMEM((CHUNK, 2 * ny, ny), BF16),
            pltpu.VMEM((nx, 2 * ny), BF16),
            pltpu.VMEM((STEPS * nx, ny), F32),
            pltpu.VMEM((n, 8, slots), F32),
            pltpu.VMEM((n, 8, slots), F32),
            dma((4 + STEPS,)),
            dma((2 * chunks,)),
            dma((2 * STEPS * chunks,)),
            dma((2 * STEPS * chunks,)),
            dma((2 * STEPS * chunks,)),
            dma((2 * STEPS * chunks,)),
            dma((n,)),
            dma((n,)),
        ],
        compiler_params=pltpu.CompilerParams(
            collective_id=0, has_side_effects=True, vmem_limit_bytes=60 * 1024 * 1024
        ),
        name="adjoint_steps",
    )(
        signs,
        rec_owner.reshape(1, recv_dev),
        rec_cell.reshape(1, recv_dev),
        jnp.asarray(step_table(NT, STEPS)),
        p_prev, p_cur, courant, snapshots, residual,
    )


def solution(mesh):
    placed = (
        P(None, "gx", "gy"),
        P(None, "gx", "gy"),
        P(None, "gx", "gy"),
        P(None, None, "gx", "gy"),
        P(None, ("gx", "gy"), None),
        P(("gx", "gy"), None),
        P(("gx", "gy")),
        P(),
    )
    return jax.shard_map(
        functools.partial(shards, mesh.shape["gx"], mesh.shape["gy"]),
        mesh=mesh,
        in_specs=placed,
        out_specs=(P(None, "gx", "gy"), P(None, "gx", "gy")),
        check_vma=False,
    )
```

time: 378 us -> 50.1 us (0.13)
  the two profiles are of different devices: /device:TPU:12 before, /device:TPU:0 now
where the time goes in v1:
time: 50.1 us; the launch traced here: 49.9 us
  Pallas kernels  43.5 us (87%)
  local copies, waits for them, and re-layouts  5.73 us (11%)
  between operations  0.65 us (1%)
    pallas_call x1, Pallas kernels, shards(): pl.pallas_call(functools.partial(kernel, n_gx, n_gy), out_shape=(whole, w...  43.5 us
    unnamed x4, local copies, waits for them, and re-layouts  5.73 us

profile of v1, /device:TPU:0, one launch (start us, length us, event | category | flops | bytes accessed | tf_op | source)
XLA Modules:
  0.0 49.9 jit_solution(16097615487238867789)
XLA Ops:
  0.6 43.5 %adjoint_steps.1 = (f32[48,128,128]{2,1,0:T(8,128)}, f32[48,128,128]{2,1,0:T(8,128)}) custom-call(s32[4]{0:T(128)} %signs.1, s32[1,2048]{1,0:T(1,128)} %bitcast.2, s32[1,2048]{1,0:T(1,128)} %bitcast.3, f32[8,128]{1,0:T(8,128)} %constant.2.clone.table, f32[48,128,128]{2,1,0:T(8,128)} %p_prev.1, f32[48,128,128]{2,1,0:T(8,128)} %p_cur.1, ...), custom_call_target="tpu_custom_call" | custom-call | tf_op jit(solution)/shard_map/adjoint_steps/pallas_call | solution.py:363
  44.1 0.0 copy-start
  44.1 4.1 %copy.13 = f32[48,128,128]{2,1,0:T(8,128)} copy(f32[48,128,128]{2,1,0:T(8,128)} %get-tuple-element.4) | data formatting | bytes 6291456
  48.2 0.0 copy-done
  48.2 1.7 %copy.14 = f32[48,128,128]{2,1,0:T(8,128)} copy(f32[48,128,128]{2,1,0:T(8,128)S(1)} %copy-done) | data formatting | bytes 6291456
Async XLA Ops:
  44.1 4.1 %copy-start = (f32[48,128,128]{2,1,0:T(8,128)S(1)}, f32[48,128,128]{2,1,0:T(8,128)}, u32[]{:S(2)}) copy-start(f32[48,128,128]{2,1,0:T(8,128)} %get-tuple-element.5) | copy-start | bytes 9437188

commit v2 on v1

--- a/solution.py
+++ b/solution.py
@@ -15,9 +15,10 @@
 HALO = 4
 CHUNK = 16
 BLOCK = 256
+GROUP = 4
 
 SCALE = 5040.0
-CENTER = -205.0 / 72.0 * SCALE
+CENTER_Y, CENTER_X = -43008.0, -42.0
 TAPS = (8064.0, -1008.0, 128.0, -9.0)
 
 F32 = jnp.float32
@@ -50,7 +51,7 @@
 def kernel(
     n_gx, n_gy, signs, owner, cell, table, p_prev, p_cur, courant_h, snaps_h, residual_h,
     field_out, image_out,
-    buf_a, buf_b, courant, snaps, residual, image, sx, rx, sy, ry, corner, edge, planes,
+    buf_a, buf_b, courant, snaps, residual, image, sx, rx, sy, ry, edge, planes,
     snd, got, load_sem, out_sem, sxs, rxs, sys_, rys, snds, gots,
 ):
     n = n_gx * n_gy
@@ -81,9 +82,12 @@
 
     lax.fori_loop(1, n, greet, 0)
 
-    band = taps(jnp.abs(iota((nx, nx), 0) - iota((nx, nx), 1))).astype(BF16)
-    t_x = jnp.concatenate([band, band], axis=1)
-    t_y = jnp.concatenate([band, band], axis=0) if nx == ny else None
+    def band(size, center):
+        distance = jnp.abs(iota((size, size), 0) - iota((size, size), 1))
+        return jnp.where(distance == 0, center, taps(distance)).astype(BF16)
+
+    t_x = jnp.concatenate([band(nx, CENTER_X)] * 2, axis=1)
+    t_y = jnp.concatenate([band(ny, CENTER_Y)] * 2, axis=0)
     row = iota((16, 16), 0)
     src = iota((16, 16), 1) & 7
     place = jnp.where(src < 4, src - 4, nx + src - 4)
@@ -91,16 +95,10 @@
     h_x = taps(jnp.abs(place - target)).astype(BF16)
     a, b = iota((ny, ny), 0), iota((ny, ny), 1)
     pos = jnp.where(a < mid, (a & 3) - 4, ny + (a & 3))
-    edge_taps = taps(jnp.abs(b - pos))
+    onto = jnp.where((b & 7) < 4, ny - 4 + (b & 7), (b & 7) - 4)
     group = (a & (mid - 1)) >> 2
-
-    def fill(q, carry):
-        c = jnp.where(group == q, edge_taps, 0.0).astype(BF16)
-        corner[q, pl.ds(0, ny), :] = c
-        corner[q, pl.ds(ny, ny), :] = c
-        return carry
-
-    lax.fori_loop(0, CHUNK, fill, 0)
+    e_y = jnp.where(group == (b >> 3), taps(jnp.abs(onto - pos)), 0.0).astype(BF16)
+    e_y = jnp.concatenate([e_y, e_y], axis=0)
     zero = jnp.zeros((HALO, nx, ny), F32)
     for buf in (buf_a, buf_b):
         buf[pl.ds(0, HALO)] = zero
@@ -121,6 +119,8 @@
                 ry[k, side] = jnp.zeros(ry.shape[2:], F32)
 
     lane = iota((half, ny), 1)
+    lanes = iota((nx, ny), 1)
+    outer = (lanes < 4) | (lanes >= ny - 4)
 
     def pack(v, k, g, q):
         z = g * CHUNK + q
@@ -239,38 +239,56 @@
         edges = jnp.concatenate(
             [jnp.where(near, left, right), pltpu.roll(jnp.where(near, right, left), mid, 1)], axis=0
         )
-        edge[...] = split(edges, 1)
-
-        def plane(q):
-            z = g * CHUNK + q
-            v = cur[z + HALO]
-            lap = jnp.dot(split(v, 1), t_y, preferred_element_type=F32)
-            lap = lap + jnp.dot(edge[...], corner[q], preferred_element_type=F32)
-            lap = lap + jnp.dot(t_x, split(v, 0), preferred_element_type=F32)
-            over = jnp.concatenate([rx[k, 0, z], rx[k, 1, z]], axis=0)
-            over_hi = over.astype(BF16).astype(F32)
-            over = jnp.concatenate([over_hi, over - over_hi], axis=0).astype(BF16)
-            border = jnp.dot(h_x, over, preferred_element_type=F32)
-            depth = (3.0 * CENTER) * v
-            for i in range(1, HALO + 1):
-                depth = depth + TAPS[i - 1] * (cur[z + HALO + i] + cur[z + HALO - i])
-            lap = lap + depth
-            lap = jnp.concatenate(
-                [lap[:8] + border[:8], lap[8 : nx - 8], lap[nx - 8 :] + border[8:]], axis=0
+        edge[...] = jnp.dot(split(edges, 1), e_y, preferred_element_type=F32)
+
+        def body(j, carry):
+            qs = [GROUP * j + i for i in range(GROUP)]
+            vs = [cur[g * CHUNK + q + HALO] for q in qs]
+            parts = []
+            for v in vs:
+                hi = v.astype(BF16)
+                parts.append((hi, (v - hi.astype(F32)).astype(BF16)))
+            along_y = jnp.dot(
+                jnp.concatenate([jnp.concatenate(p, axis=1) for p in parts], axis=0), t_y,
+                preferred_element_type=F32,
             )
-            nxt = (2.0 * v - prev[z + HALO]) + (courant[z] * (1.0 / SCALE)) * lap
-            prev[z + HALO] = nxt
-            shot = snaps[k, z].astype(F32) * nxt
-            image[z] = shot if k == 0 else image[z] + shot
-            if k < STEPS - 1:
-                pack(nxt, k + 1, g, q)
-
-        def body(j, carry):
-            plane(2 * j)
-            plane(2 * j + 1)
+            along_x = jnp.dot(
+                t_x, jnp.concatenate([jnp.concatenate(p, axis=0) for p in parts], axis=1),
+                preferred_element_type=F32,
+            )
+            overs = []
+            for q in qs:
+                z = g * CHUNK + q
+                over = jnp.concatenate([rx[k, 0, z], rx[k, 1, z]], axis=0)
+                over_hi = over.astype(BF16).astype(F32)
+                overs.append(jnp.concatenate([over_hi, over - over_hi], axis=0).astype(BF16))
+            border = jnp.dot(h_x, jnp.concatenate(overs, axis=1), preferred_element_type=F32)
+            for i, (q, v) in enumerate(zip(qs, vs)):
+                z = g * CHUNK + q
+                cols = slice(i * ny, (i + 1) * ny)
+                depth = TAPS[0] * (cur[z + HALO + 1] + cur[z + HALO - 1])
+                for r in range(2, HALO + 1):
+                    depth = depth + TAPS[r - 1] * (cur[z + HALO + r] + cur[z + HALO - r])
+                lap = along_y[i * nx : (i + 1) * nx] + along_x[:, cols] + depth
+                lap = lap + jnp.where(outer, pltpu.roll(edge[...], (2 * ny - 4 - 8 * q) & (ny - 1), 1), 0.0)
+                lap = jnp.concatenate(
+                    [lap[:8] + border[:8, cols], lap[8 : nx - 8], lap[nx - 8 :] + border[8:, cols]],
+                    axis=0,
+                )
+                if k == 0:
+                    speed = courant[z] * (1.0 / SCALE)
+                    courant[z] = speed
+                else:
+                    speed = courant[z]
+                nxt = (2.0 * v - prev[z + HALO]) + speed * lap
+                prev[z + HALO] = nxt
+                shot = snaps[k, z].astype(F32) * nxt
+                image[z] = shot if k == 0 else image[z] + shot
+                if k < STEPS - 1:
+                    pack(nxt, k + 1, g, q)
             return carry
 
-        lax.fori_loop(0, CHUNK // 2, body, 0)
+        lax.fori_loop(0, CHUNK // GROUP, body, 0)
         if k < STEPS - 1:
             send_halo(k + 1, g)
 
@@ -317,7 +335,8 @@
                 if k == 0:
                     scatter()
                 at = HALO + RECV_DEPTH
-                prev[at] = prev[at] - courant[RECV_DEPTH] * planes[pl.ds(k * nx, nx), :]
+                speed = courant[RECV_DEPTH] * (1.0 if k == 0 else SCALE)
+                prev[at] = prev[at] - speed * planes[pl.ds(k * nx, nx), :]
             step_chunk(k, g, cur, prev)
             if k == STEPS - 1:
                 zs = pl.ds(g * CHUNK, CHUNK)
@@ -376,8 +395,7 @@
             pltpu.VMEM((STEPS, 2, nz, HALO, ny), F32),
             pltpu.VMEM((STEPS, 2, chunks, nx // 2, ny), F32),
             pltpu.VMEM((STEPS, 2, chunks, nx // 2, ny), F32),
-            pltpu.VMEM((CHUNK, 2 * ny, ny), BF16),
-            pltpu.VMEM((nx, 2 * ny), BF16),
+            pltpu.VMEM((nx, ny), F32),
             pltpu.VMEM((STEPS * nx, ny), F32),
             pltpu.VMEM((n, 8, slots), F32),
             pltpu.VMEM((n, 8, slots), F32),

time: 50.1 us -> 43.2 us (0.86)
  Pallas kernels: 43.5 us -> 36.7 us
    pallas_call x1, Pallas kernels: 43.5 us -> 36.7 us  [shards(): pl.pallas_call(functools.partial(kernel, n_gx, n_gy), out_shape=(whole, w...]
where the time goes in v2:
time: 43.2 us; the launch traced here: 43.1 us
  Pallas kernels  36.7 us (85%)
  local copies, waits for them, and re-layouts  5.73 us (13%)
  between operations  0.65 us (2%)
    pallas_call x1, Pallas kernels, shards(): pl.pallas_call(functools.partial(kernel, n_gx, n_gy), out_shape=(whole, w...  36.7 us
    unnamed x4, local copies, waits for them, and re-layouts  5.73 us

profile of v2, /device:TPU:0, one launch (start us, length us, event | category | flops | bytes accessed | tf_op | source)
XLA Modules:
  0.0 43.1 jit_solution(1367743424332426562)
XLA Ops:
  0.6 36.7 %adjoint_steps.1 = (f32[48,128,128]{2,1,0:T(8,128)}, f32[48,128,128]{2,1,0:T(8,128)}) custom-call(s32[4]{0:T(128)} %signs.1, s32[1,2048]{1,0:T(1,128)} %bitcast.2, s32[1,2048]{1,0:T(1,128)} %bitcast.3, f32[8,128]{1,0:T(8,128)} %constant.2.clone.table, f32[48,128,128]{2,1,0:T(8,128)} %p_prev.1, f32[48,128,128]{2,1,0:T(8,128)} %p_cur.1, ...), custom_call_target="tpu_custom_call" | custom-call | tf_op jit(solution)/shard_map/adjoint_steps/pallas_call | solution.py:382
  37.3 0.0 copy-start
  37.3 4.1 %copy.13 = f32[48,128,128]{2,1,0:T(8,128)} copy(f32[48,128,128]{2,1,0:T(8,128)} %get-tuple-element.4) | data formatting | bytes 6291456
  41.4 0.0 copy-done
  41.4 1.7 %copy.14 = f32[48,128,128]{2,1,0:T(8,128)} copy(f32[48,128,128]{2,1,0:T(8,128)S(1)} %copy-done) | data formatting | bytes 6291456
Async XLA Ops:
  37.3 4.1 %copy-start = (f32[48,128,128]{2,1,0:T(8,128)S(1)}, f32[48,128,128]{2,1,0:T(8,128)}, u32[]{:S(2)}) copy-start(f32[48,128,128]{2,1,0:T(8,128)} %get-tuple-element.5) | copy-start | bytes 9437188
